TPU v7x, 32 devices: a whole 2x2x4 slice. The times are simulated.
32 devices in a mesh: grp: 4 (over y, x), slab: 8 (over z, core).
Axes of the slice: x: 2, y: 2, z: 4, core: 2. Of those that a mesh axis runs over, the one named last changes fastest.
Arguments:
- fields: float32 [64, 64, 8, 128], P('grp', 'slab'), may hold values from -6 to 6
- velocity: int32 [3, 64, 8, 128], P(None, 'slab'), may hold values from -2 to 2
- diffusivity: float32 [64, 8, 128], P('slab'), may hold values from 0.005 to 0.04
- sensor_offsets: int32 [49152], P('slab'), may hold values from 0 to 8191
- sensor_counts: int32 [8], P('slab'), may hold values from 1 to 6144, 16384 in all
- observations: float32 [49152], P('slab'), may hold values from -6 to 6
- noise_scale: float32 [49152], P('slab'), may hold values from 2 to 20
- perturbation: float32 [64, 49152], P('grp', 'slab'), may hold values from -6 to 6
Outputs:
- updated: float32 [64, 64, 8, 128], P('grp', 'slab')
Inputs may be any that keep to these rules, and one draw needn't show every extreme that they name: `sensor_counts`: the counts sum to 16384 and the largest is exactly 6144. `sensor_offsets`: slots at or past their slab's count are unused.
All inputs are finite; a program needn't handle non-finite values. No bound on the sum of `sensor_counts` on one device may be relied on, other than what follows from the above.
Results may differ from a plain program's by a relative error of at most 0.00011.
Values sent between devices are 32-bit elements; how exact they have to be, the bound alone decides.
A program may use at most 64 MiB of HBM per device.

v0:
```python
import math
import jax
import jax.numpy as jnp
from jax import lax
from jax.sharding import PartitionSpec as P

STEPS = 2
COURANT = 0.12


def extended_2(array, sides, width):
    for axis, dim in sides:
        size, length = (lax.axis_size(axis), array.shape[dim])
        up = [(i, (i + 1) % size) for i in range(size - 1)]
        down = [(j, i) for i, j in up]
        last = lax.slice_in_dim(array, length - width, length, axis=dim)
        initial = lax.slice_in_dim(array, 0, width, axis=dim)
        before = lax.ppermute(last, axis, up)
        after = lax.ppermute(initial, axis, down)
        array = jnp.concatenate([before, array, after], axis=dim)
    return array


def upwind(courant, center, lower_side, upper_side):
    return jnp.maximum(courant, 0.0) * (center - lower_side) + jnp.minimum(courant, 0.0) * (
        upper_side - center
    )


def advance(extended, courant, diffusivity):
    center = extended[:, 1:-1]
    below = extended[:, :-2]
    above = extended[:, 2:]
    south = jnp.roll(center, 1, axis=2)
    north = jnp.roll(center, -1, axis=2)
    west = jnp.roll(center, 1, axis=3)
    east = jnp.roll(center, -1, axis=3)
    transport = upwind(courant[0], center, below, above) + upwind(courant[1], center, south, north)
    transport = transport + upwind(courant[2], center, west, east)
    laplace = below + above + south + north + west + east - 6.0 * center
    return center - transport + diffusivity * laplace


def solve_weights(gram_matrix, cross_matrix, spread_root):
    order = gram_matrix.shape[0]
    index_row = jnp.arange(order, dtype=jnp.int32)
    system = jnp.eye(order, dtype=jnp.float32) + gram_matrix

    def factor_column(column, lower_factor):
        row_here = lax.dynamic_slice_in_dim(lower_factor, column, 1, 0)[0]
        needed = lax.dynamic_slice_in_dim(system, column, 1, 1)[:, 0]
        needed = needed - jnp.dot(
            lower_factor,
            row_here,
            precision=lax.Precision.HIGHEST,
            preferred_element_type=jnp.float32,
        )
        pivot = jnp.sqrt(lax.dynamic_slice_in_dim(needed, column, 1, 0)[0])
        values = jnp.where(index_row >= column, needed / pivot, 0.0)
        marker = (index_row == column).astype(jnp.float32)
        return lower_factor + values[:, None] * marker[None, :]

    lower_factor = lax.fori_loop(0, order, factor_column, jnp.zeros((order, order), jnp.float32))

    def forward_row(row, solved):
        factor_row = lax.dynamic_slice_in_dim(lower_factor, row, 1, 0)[0]
        pivot = lax.dynamic_slice_in_dim(factor_row, row, 1, 0)[0]
        given = lax.dynamic_slice_in_dim(cross_matrix, row, 1, 0)[0]
        value = (
            given
            - jnp.dot(
                factor_row,
                solved,
                precision=lax.Precision.HIGHEST,
                preferred_element_type=jnp.float32,
            )
        ) / pivot
        return lax.dynamic_update_slice_in_dim(solved, value[None, :], row, 0)

    middle = lax.fori_loop(0, order, forward_row, jnp.zeros_like(cross_matrix))

    def backward_row(turn, solved):
        row = order - 1 - turn
        factor_col = lax.dynamic_slice_in_dim(lower_factor, row, 1, 1)[:, 0]
        pivot = lax.dynamic_slice_in_dim(factor_col, row, 1, 0)[0]
        given = lax.dynamic_slice_in_dim(middle, row, 1, 0)[0]
        value = (
            given
            - jnp.dot(
                factor_col,
                solved,
                precision=lax.Precision.HIGHEST,
                preferred_element_type=jnp.float32,
            )
        ) / pivot
        return lax.dynamic_update_slice_in_dim(solved, value[None, :], row, 0)

    result = lax.fori_loop(0, order, backward_row, jnp.zeros_like(cross_matrix))
    return result / spread_root


def ensemble_parts(centered, misfit_rows):
    gram_part = jnp.dot(
        centered, centered.T, precision=lax.Precision.HIGHEST, preferred_element_type=jnp.float32
    )
    cross_part = jnp.dot(
        centered, misfit_rows.T, precision=lax.Precision.HIGHEST, preferred_element_type=jnp.float32
    )
    return (gram_part, cross_part)


def sample_cells(current, sensor_offsets):
    members_here = current.shape[0]
    row_count = current.shape[1] * current.shape[2]
    width = current.shape[3]
    planes = current.reshape(members_here, row_count, width)
    slot_total = sensor_offsets.shape[0]
    block_size = math.gcd(slot_total, 512)
    block_count = slot_total // block_size
    row_ids = jnp.arange(row_count, dtype=jnp.int32)
    col_ids = jnp.arange(width, dtype=jnp.int32)

    def pick_block(offsets):
        row_pick = offsets // width
        col_pick = offsets % width
        col_table = (col_ids[:, None] == col_pick[None, :]).astype(jnp.float32)
        chosen = jnp.einsum(
            "qng,gl->qnl",
            planes,
            col_table,
            precision=lax.Precision.HIGHEST,
            preferred_element_type=jnp.float32,
        )
        row_table = (row_ids[:, None] == row_pick[None, :]).astype(jnp.float32)
        return jnp.sum(chosen * row_table[None, :, :], axis=1)

    blocks = lax.map(pick_block, sensor_offsets.reshape(block_count, block_size))
    return jnp.transpose(blocks, (1, 0, 2)).reshape(members_here, slot_total)


def local(
    fields,
    velocity,
    diffusivity,
    sensor_offsets,
    sensor_counts,
    observations,
    noise_scale,
    perturbation,
):
    members_here = fields.shape[0]
    group_count = lax.axis_size("grp")
    members_all = members_here * group_count
    spread_root = math.sqrt(members_all - 1)
    courant = velocity.astype(jnp.float32) * COURANT
    current = fields
    for counter in range(STEPS):
        extended = extended_2(current, (("slab", 1),), 1)
        current = advance(extended, courant, diffusivity)
    cell_total = current.shape[1] * current.shape[2] * current.shape[3]
    flattened = current.reshape(members_here, cell_total)
    slot_total = sensor_offsets.shape[0]
    live_mask = (jnp.arange(slot_total, dtype=jnp.int32) < sensor_counts[0]).astype(jnp.float32)
    predicted = sample_cells(current, sensor_offsets)
    scaled = live_mask * predicted / noise_scale
    misfit = live_mask * ((observations - predicted) / noise_scale + perturbation)
    scaled_sum = lax.psum(jnp.sum(scaled, axis=0), "grp")
    leading = (scaled - scaled_sum / members_all) / spread_root
    gathered_lead, gathered_misfit = (
        lax.all_gather(leading, "grp", axis=0, tiled=True),
        lax.all_gather(misfit, "grp", axis=0, tiled=True),
    )
    gram_part, cross_part = ensemble_parts(gathered_lead, gathered_misfit)
    gram_matrix, cross_matrix = lax.psum((gram_part, cross_part), "slab")
    weights = solve_weights(gram_matrix, cross_matrix, spread_root)
    group_index = lax.axis_index("grp")
    own_weights = lax.dynamic_slice_in_dim(weights, group_index * members_here, members_here, 1)
    increment = jnp.dot(
        own_weights.T,
        lax.all_gather(flattened, "grp", axis=0, tiled=True),
        precision=lax.Precision.HIGHEST,
        preferred_element_type=jnp.float32,
    )
    return (flattened + increment).reshape(current.shape)


def solution(mesh):
    return jax.shard_map(
        local,
        mesh=mesh,
        in_specs=(
            P("grp", "slab", None, None),
            P(None, "slab", None, None),
            P("slab", None, None),
            P("slab"),
            P("slab"),
            P("slab"),
            P("slab"),
            P("grp", "slab"),
        ),
        out_specs=P("grp", "slab", None, None),
        check_vma=False,
    )
```

profile of v0, /device:TPU:0, one launch (start us, length us, event | category | flops | bytes accessed | tf_op | source)
XLA Modules:
  0.0 487.9 jit_solution(3557998516879532501)
XLA Ops:
  6.5 1.6 fusion.75
  8.1 3.0 collective-permute-start
  11.1 1.3 collective-permute-start.1
  12.4 1.3 fusion.72
  17.3 1.3 reshape.81
  19.9 1.4 div.111
  21.9 2.0 fusion.51
  24.5 4.6 collective-permute-start.2
  29.1 1.3 collective-permute-start.3
  30.5 3.0 collective-permute-done.3
  34.4 31.0 %while.62 = (s32[]{:T(128)}, f32[12,16,512]{2,1,0:T(8,128)S(1)}, s32[12,512]{1,0:T(8,128)}, f32[16,64,128]{2,1,0:T(8,128)S(1)}, s32[]{:T(128)}) while((s32[]{:T(128)}, f32[12,16,512]{2,1,0:T(8,128)S(1)}, s32[12,512]{1,0:T(8,128)}, f32[16,64,128]{2,1,0:T(8,128)S(1)}, s32[]{:T(128)}) %tuple.168), condition=%wide.region_2.3_spmd.clone, body=%wide.region_0.2_spmd.clone.sunk | while | flops 806489600 | bytes 901193 | solution.py:137
  48.9 1.1 fusion.109
  59.2 1.1 fusion.109
  65.7 16.3 %psum.21 = f32[6144]{0:T(1024)S(1)} all-reduce(f32[6144]{0:T(1024)S(1)} %reduce_sum.24), channel_id=1, replica_groups=mesh['grp'=4,'slab'=8] {'grp'}, use_global_device_ids=true, to_apply=%region_4.5 | all-reduce | flops 6144 | bytes 49152 | tf_op jit(solution)/shard_map/psum | solution.py:167
  83.8 1.1 copy.20
  85.0 29.7 %all-gather.4.cloned.1.call-done = f32[64,6144]{1,0:T(8,128)} async-done(((f32[16,6144]{1,0:T(8,128)}), f32[64,6144]{1,0:T(8,128)}) %all-gather.4.cloned.1.call-update) | async-done | bytes 1572880 | tf_op jit(solution)/shard_map/all_gather | solution.py:170
  114.6 3.4 fusion.77
  118.0 29.3 %all-gather.6.cloned.1.call-done = f32[64,6144]{1,0:T(8,128)} async-done(((f32[16,6144]{1,0:T(8,128)}), f32[64,6144]{1,0:T(8,128)}) %all-gather.6.cloned.1.call-update) | async-done | bytes 1572880 | tf_op jit(solution)/shard_map/all_gather | solution.py:171
  147.3 2.8 fusion.76
  150.1 28.9 %all-reduce = (f32[64,64]{1,0:T(8,128)S(1)}, f32[64,64]{1,0:T(8,128)S(1)}) all-reduce(f32[64,64]{1,0:T(8,128)S(1)} %fusion.76, f32[64,64]{1,0:T(8,128)S(1)} %fusion.77), channel_id=1, replica_groups=mesh['grp'=4,'slab'=8] {'slab'}, use_global_device_ids=true, to_apply=%region_8.9 | all-reduce | flops 8192 | bytes 65536 | tf_op jit(solution)/shard_map/psum | solution.py:174
  179.1 105.9 %while.63 = (s32[]{:T(128)}, f32[64,64]{1,0:T(8,128)S(1)}, f32[64,64]{0,1:T(8,128)S(1)}, s32[]{:T(128)}, s32[]{:T(128)}) while((s32[]{:T(128)}, f32[64,64]{1,0:T(8,128)S(1)}, f32[64,64]{0,1:T(8,128)S(1)}, s32[]{:T(128)}, s32[]{:T(128)}) %tuple.153), condition=%wide.region_7.8_spmd.clone.clone, body=%wide.region_6.7_spmd.clone.clone.sunk | while | flops 65923 | bytes 101992 | solution.py:63
  285.1 96.0 %while.60 = (s32[]{:T(128)}, f32[64,64]{1,0:T(8,128)S(1)}, f32[64,64]{1,0:T(8,128)S(1)}, f32[64,64]{1,0:T(8,128)S(1)}, s32[]{:T(128)}, /*index=5*/s32[]{:T(128)}, s32[]{:T(128)}) while((s32[]{:T(128)}, f32[64,64]{1,0:T(8,128)S(1)}, f32[64,64]{1,0:T(8,128)S(1)}, f32[64,64]{1,0:T(8,128)S(1)}, s32[]{:T(128)}, /*index=5*/s32[]{:T(128)}, ...), condition=%wide.region_10.11_spmd, body=%wide.region_9.10_spmd.sunk | while | flops 49283 | bytes 36205 | solution.py:80
  381.1 96.4 %while.61 = (s32[]{:T(128)}, f32[64,64]{1,0:T(8,128)S(1)}, f32[64,64]{1,0:T(8,128)S(1)}, f32[64,64]{0,1:T(8,128)S(1)}, s32[]{:T(128)}, /*index=5*/s32[]{:T(128)}, s32[]{:T(128)}, s32[]{:T(128)}) while((s32[]{:T(128)}, f32[64,64]{1,0:T(8,128)S(1)}, f32[64,64]{1,0:T(8,128)S(1)}, f32[64,64]{0,1:T(8,128)S(1)}, s32[]{:T(128)}, ...), condition=%wide.region_12.13_spmd, body=%wide.region_11.12_spmd.sunk | while | flops 49287 | bytes 35751 | solution.py:98
  477.6 2.9 fusion.26
  (892 shorter events, 286.0 us)
Async XLA Ops:
  6.5 7.2 %copy-start = (f32[16,8,8,128]{3,2,1,0:T(8,128)S(1)}, f32[16,8,8,128]{3,2,1,0:T(8,128)}, u32[]{:S(2)}) copy-start(f32[16,8,8,128]{3,2,1,0:T(8,128)} %param.16) | copy-start | bytes 1572868
  6.5 108.1 %all-gather.4.cloned.1.call-start = ((), (), s32[]{:S(2)}) async-start(), calls=%async_computation | async-start | bytes 1966080 | tf_op jit(solution)/shard_map/all_gather | solution.py:170
  8.1 13.8 %collective-permute-start = (f32[16,1,8,128]{3,2,1,0:T(8,128)}, f32[16,1,8,128]{3,2,1,0:T(8,128)}, u32[]{:S(2)}, u32[]{:S(2)}) collective-permute-start(f32[16,1,8,128]{3,2,1,0:T(8,128)} %get-tuple-element.525), channel_id=1, source_target_pairs={{0,1},{1,2},{2,3},{3,4},{4,5},{5,6},{6,7},{8,9},{9,10},{10,11},{11... | collective-permute-start | bytes 196616 | tf_op jit(solution)/shard_map/ppermute | solution.py:18
  11.1 10.7 %collective-permute-start.1 = (f32[16,1,8,128]{3,2,1,0:T(8,128)}, f32[16,1,8,128]{3,2,1,0:T(8,128)}, u32[]{:S(2)}, u32[]{:S(2)}) collective-permute-start(f32[16,1,8,128]{3,2,1,0:T(8,128)} %get-tuple-element.526), channel_id=1, source_target_pairs={{1,0},{2,1},{3,2},{4,3},{5,4},{6,5},{7,6},{9,8},{10,9},{11,10},{12... | collective-permute-start | bytes 196616 | tf_op jit(solution)/shard_map/ppermute | solution.py:19
  24.2 9.3 %copy-start.3 = (f32[8,8,128]{2,1,0:T(8,128)S(1)}, f32[8,8,128]{2,1,0:T(8,128)}, u32[]{:S(2)}) copy-start(f32[8,8,128]{2,1,0:T(8,128)} %get-tuple-element.529) | copy-start | bytes 98308
  24.2 9.3 %copy-start.4 = (f32[8,8,128]{2,1,0:T(8,128)S(1)}, f32[8,8,128]{2,1,0:T(8,128)}, u32[]{:S(2)}) copy-start(f32[8,8,128]{2,1,0:T(8,128)} %get-tuple-element.530) | copy-start | bytes 98308
  24.2 9.3 %copy-start.5 = (f32[8,8,128]{2,1,0:T(8,128)S(1)}, f32[8,8,128]{2,1,0:T(8,128)}, u32[]{:S(2)}) copy-start(f32[8,8,128]{2,1,0:T(8,128)} %get-tuple-element.531) | copy-start | bytes 98308
  24.2 9.3 %copy-start.6 = (f32[8,8,128]{2,1,0:T(8,128)S(1)}, f32[8,8,128]{2,1,0:T(8,128)}, u32[]{:S(2)}) copy-start(f32[8,8,128]{2,1,0:T(8,128)} %get-tuple-element.532) | copy-start | bytes 98308
  24.3 9.3 %copy-start.7 = (f32[8,8,128]{2,1,0:T(8,128)S(1)}, f32[8,8,128]{2,1,0:T(8,128)}, u32[]{:S(2)}) copy-start(f32[8,8,128]{2,1,0:T(8,128)} %get-tuple-element.533) | copy-start | bytes 98308
  24.3 9.3 %copy-start.8 = (f32[8,8,128]{2,1,0:T(8,128)S(1)}, f32[8,8,128]{2,1,0:T(8,128)}, u32[]{:S(2)}) copy-start(f32[8,8,128]{2,1,0:T(8,128)} %get-tuple-element.534) | copy-start | bytes 98308
  24.3 9.3 %copy-start.9 = (f32[8,8,128]{2,1,0:T(8,128)S(1)}, f32[8,8,128]{2,1,0:T(8,128)}, u32[]{:S(2)}) copy-start(f32[8,8,128]{2,1,0:T(8,128)} %param.18) | copy-start | bytes 98308
  24.5 6.0 %collective-permute-start.2 = (f32[16,1,8,128]{3,2,1,0:T(8,128)S(1)}, f32[16,1,8,128]{3,2,1,0:T(8,128)S(1)}, u32[]{:S(2)}, u32[]{:S(2)}) collective-permute-start(f32[16,1,8,128]{3,2,1,0:T(8,128)S(1)} %get-tuple-element.515), channel_id=1, source_target_pairs={{0,1},{1,2},{2,3},{3,4},{4,5},{5,6},{6,7},{8,9},{9,10},{10,11},{11... | collective-permute-start | bytes 196616 | tf_op jit(solution)/shard_map/ppermute | solution.py:18
  29.1 4.4 collective-permute-start.3
  34.4 31.1 %copy-start.10 = (f32[12,512]{1,0:T(8,128)S(1)}, f32[12,512]{1,0:T(8,128)}, u32[]{:S(2)}) copy-start(f32[12,512]{1,0:T(8,128)} %fusion.61) | copy-start | bytes 73732
  34.4 31.1 %copy-start.11 = (f32[12,512]{1,0:T(8,128)S(1)}, f32[12,512]{1,0:T(8,128)}, u32[]{:S(2)}) copy-start(f32[12,512]{1,0:T(8,128)} %div.111) | copy-start | bytes 73732
  34.4 47.5 %copy-start.12 = (f32[6144]{0:T(1024)S(1)}, f32[6144]{0:T(1024)}, u32[]{:S(2)}) copy-start(f32[6144]{0:T(1024)} %param.22) | copy-start | bytes 73732
  34.4 47.5 %copy-start.13 = (f32[6144]{0:T(1024)S(1)}, f32[6144]{0:T(1024)}, u32[]{:S(2)}) copy-start(f32[6144]{0:T(1024)} %fusion.62) | copy-start | bytes 73732
  34.4 47.5 %copy-start.14 = (f32[6144]{0:T(1024)S(1)}, f32[6144]{0:T(1024)}, u32[]{:S(2)}) copy-start(f32[6144]{0:T(1024)} %param.21) | copy-start | bytes 73732
  65.5 16.5 %copy-start.2 = (f32[16,6144]{1,0:T(8,128)S(1)}, f32[16,6144]{1,0:T(8,128)}, u32[]{:S(2)}) copy-start(f32[16,6144]{1,0:T(8,128)} %param.23) | copy-start | bytes 1179652
  83.0 64.3 %all-gather.6.cloned.1.call-start = ((), (), s32[]{:S(2)}) async-start(), calls=%async_computation.1 | async-start | bytes 1966080 | tf_op jit(solution)/shard_map/all_gather | solution.py:171
  83.8 393.8 %all-gather.8.cloned.1.call-start = ((), (), s32[]{:S(2)}) async-start(), calls=%async_computation.2 | async-start | bytes 2621440 | tf_op jit(solution)/shard_map/all_gather | solution.py:180
  114.6 32.7 %copy-start.1 = (f32[64,6144]{1,0:T(8,128)S(1)}, f32[64,6144]{1,0:T(8,128)}, u32[]{:S(2)}) copy-start(f32[64,6144]{1,0:T(8,128)} %all-gather.4.cloned.1.call-done) | copy-start | bytes 4718596
Sparse Core Ops, SparseCore 0:
  83.1 31.4 all-gather.3
  116.5 30.8 all-gather.5
  149.2 35.2 all-gather.7
where the time goes:
time: 492 us; the launch traced here: 488 us
  local copies, waits for them, and re-layouts  140 us (28%)
  matrix products  134 us (27%)
  waiting for transfers between devices  62.7 us (13%)
  loops' own time  50.6 us (10%)
  blocking collectives  45.2 us (9%)
  other arithmetic  30.7 us (6%)
  between operations  14.2 us (3%)
  starting transfers between devices  10.3 us (2%)
    dot_general x64, matrix products, forward_row(): jnp.dot(factor_row, solved, precision=lax.Precision.HIGHEST, preferred_el...  51.5 us
    dot_general x64, matrix products, backward_row(): jnp.dot(factor_col, solved, precision=lax.Precision.HIGHEST, preferred_el...  51.5 us
    another operation x1, loops' own time, solve_weights(): lax.fori_loop(0, order, factor_column, jnp.zeros((order, order), jnp.floa...  47.1 us
    dynamic_slice x64, local copies, waits for them, and re-layouts, factor_column(): pivot = jnp.sqrt(lax.dynamic_slice_in_dim(needed, column, 1, 0)[0])  43.5 us
    dynamic_slice x64, local copies, waits for them, and re-layouts, forward_row(): pivot = lax.dynamic_slice_in_dim(factor_row, row, 1, 0)[0]  41.6 us
    dynamic_slice x64, local copies, waits for them, and re-layouts, backward_row(): pivot = lax.dynamic_slice_in_dim(factor_col, row, 1, 0)[0]  41.6 us
    all_gather x1, waiting for transfers between devices, local(): lax.all_gather(leading, 'grp', axis=0, tiled=True)  29.7 us
    all_gather x1, waiting for transfers between devices, local(): lax.all_gather(misfit, 'grp', axis=0, tiled=True)  29.3 us
  transfers between devices with their start and end apart: 7, of which 3 were waited for; matrix products, arithmetic and copies ran while one was open for 54% of the time, Pallas kernels for 0%

commit v1 on v0

--- a/solution.py
+++ b/solution.py
@@ -3,9 +3,18 @@
 import jax.numpy as jnp
 from jax import lax
 from jax.sharding import PartitionSpec as P
+from jax.lax import axis_index, axis_size, ppermute
 
 STEPS = 2
 COURANT = 0.12
+
+
+def link_rounds(local_block, ndim_at):
+    local_block = jnp.moveaxis(local_block, 0, ndim_at)
+    work_now = local_block.shape
+    return local_block.reshape(
+        *work_now[:ndim_at], work_now[ndim_at] * work_now[ndim_at + 1], *work_now[ndim_at + 2 :]
+    )
 
 
 def extended_2(array, sides, width):
@@ -148,6 +157,17 @@
     noise_scale,
     perturbation,
 ):
+
+    def spots_run(xx, which_axis, dim_no):
+        size_here = axis_size(which_axis)
+        row_list = [(c, (c + 1) % size_here) for c in range(size_here)]
+        rows = [xx]
+        while len(rows) < size_here:
+            rows.append(ppermute(rows[-1], which_axis, perm=row_list))
+        taken_in = axis_index(which_axis)
+        rows = jnp.stack(rows, axis=0)[(taken_in - jnp.arange(size_here)) % size_here]
+        return link_rounds(rows, dim_no)
+
     members_here = fields.shape[0]
     group_count = lax.axis_size("grp")
     members_all = members_here * group_count
@@ -168,7 +188,7 @@
     leading = (scaled - scaled_sum / members_all) / spread_root
     gathered_lead, gathered_misfit = (
         lax.all_gather(leading, "grp", axis=0, tiled=True),
-        lax.all_gather(misfit, "grp", axis=0, tiled=True),
+        spots_run(misfit, "grp", 0),
     )
     gram_part, cross_part = ensemble_parts(gathered_lead, gathered_misfit)
     gram_matrix, cross_matrix = lax.psum((gram_part, cross_part), "slab")

time: 492 us -> 460 us (0.935)
  waiting for transfers between devices: 62.7 us -> 45.1 us
  matrix products: 134 us -> 128 us
  local copies, waits for them, and re-layouts: 140 us -> 134 us
    ppermute x0 -> x3, waiting for transfers between devices: none -> 42 us  [spots_run(): rows.append(ppermute(rows[-1], which_axis, perm=row_list))]
    all_gather x1, waiting for transfers between devices: 29.7 us -> 0.02 us  [local(): lax.all_gather(leading, 'grp', axis=0, tiled=True)]
    all_gather x1 -> x0, waiting for transfers between devices: 29.3 us -> none  [local(): lax.all_gather(misfit, 'grp', axis=0, tiled=True)]
  transfers between devices with their start and end apart: 7 -> 9, of which waited for: 3 -> 4; matrix products, arithmetic and copies ran while one was open for 54% -> 56% of each run, Pallas kernels for 0% -> 0%
where the time goes in v1:
time: 460 us; the launch traced here: 455 us
  local copies, waits for them, and re-layouts  134 us (29%)
  matrix products  128 us (28%)
  loops' own time  48.4 us (11%)
  waiting for transfers between devices  45.1 us (10%)
  blocking collectives  42.9 us (9%)
  other arithmetic  31.8 us (7%)
  between operations  14.5 us (3%)
  starting transfers between devices  10.3 us (2%)
    dot_general x64, matrix products, forward_row(): jnp.dot(factor_row, solved, precision=lax.Precision.HIGHEST, preferred_el...  49.3 us
    dot_general x64, matrix products, backward_row(): jnp.dot(factor_col, solved, precision=lax.Precision.HIGHEST, preferred_el...  49.3 us
    another operation x1, loops' own time, solve_weights(): lax.fori_loop(0, order, factor_column, jnp.zeros((order, order), jnp.floa...  44.9 us
    ppermute x3, waiting for transfers between devices, spots_run(): rows.append(ppermute(rows[-1], which_axis, perm=row_list))  42 us
    dynamic_slice x64, local copies, waits for them, and re-layouts, factor_column(): pivot = jnp.sqrt(lax.dynamic_slice_in_dim(needed, column, 1, 0)[0])  41 us
    dynamic_slice x64, local copies, waits for them, and re-layouts, forward_row(): pivot = lax.dynamic_slice_in_dim(factor_row, row, 1, 0)[0]  39.1 us
    dynamic_slice x64, local copies, waits for them, and re-layouts, backward_row(): pivot = lax.dynamic_slice_in_dim(factor_col, row, 1, 0)[0]  39.1 us
    psum x1, blocking collectives, local(): gram_matrix, cross_matrix = lax.psum((gram_part, cross_part), 'slab')  26.5 us
  transfers between devices with their start and end apart: 9, of which 4 were waited for; matrix products, arithmetic and copies ran while one was open for 56% of the time, Pallas kernels for 0%

profile of v1, /device:TPU:0, one launch (start us, length us, event | category | flops | bytes accessed | tf_op | source)
XLA Modules:
  0.0 454.7 jit_solution(2769471679710333137)
XLA Ops:
  6.5 1.6 fusion.77
  8.1 3.0 collective-permute-start
  11.1 1.3 collective-permute-start.1
  12.4 1.3 fusion.74
  17.3 1.3 reshape.133
  19.9 1.3 div.111
  21.8 2.0 fusion.51
  24.5 4.6 %collective-permute-start.2 = (f32[16,1,8,128]{3,2,1,0:T(8,128)S(1)}, f32[16,1,8,128]{3,2,1,0:T(8,128)S(1)}, u32[]{:S(2)}, u32[]{:S(2)}) collective-permute-start(f32[16,1,8,128]{3,2,1,0:T(8,128)S(1)} %get-tuple-element.515), channel_id=1, source_target_pairs={{0,1},{1,2},{2,3},{3,4},{4,5},{5,6},{6,7},{8,9},{9,10},{10,11},{11... | collective-permute-start | bytes 196616 | tf_op jit(solution)/shard_map/ppermute | solution.py:27
  29.1 1.3 collective-permute-start.3
  30.5 3.0 collective-permute-done.3
  34.4 31.0 %while.62 = (s32[]{:T(128)}, f32[12,16,512]{2,1,0:T(8,128)S(1)}, s32[12,512]{1,0:T(8,128)}, f32[16,64,128]{2,1,0:T(8,128)S(1)}, s32[]{:T(128)}) while((s32[]{:T(128)}, f32[12,16,512]{2,1,0:T(8,128)S(1)}, s32[12,512]{1,0:T(8,128)}, f32[16,64,128]{2,1,0:T(8,128)S(1)}, s32[]{:T(128)}) %tuple.166), condition=%wide.region_2.3_spmd.clone, body=%wide.region_0.2_spmd.clone.sunk | while | flops 806489600 | bytes 901193 | solution.py:146
  65.7 16.4 %psum.21 = f32[6144]{0:T(1024)S(1)} all-reduce(f32[6144]{0:T(1024)S(1)} %reduce_sum.24), channel_id=1, replica_groups=mesh['grp'=4,'slab'=8] {'grp'}, use_global_device_ids=true, to_apply=%region_4.5 | all-reduce | flops 6144 | bytes 49152 | tf_op jit(solution)/shard_map/psum | solution.py:187
  83.1 11.2 %collective-permute-done.4 = f32[16,6144]{1,0:T(8,128)S(1)} collective-permute-done((f32[16,6144]{1,0:T(8,128)S(1)}, f32[16,6144]{1,0:T(8,128)S(1)}, u32[]{:S(2)}, u32[]{:S(2)}) %collective-permute-start.4) | collective-permute-done | bytes 393248 | tf_op jit(solution)/shard_map/ppermute | solution.py:166
  94.3 13.2 %collective-permute-done.5 = f32[16,6144]{1,0:T(8,128)S(1)} collective-permute-done((f32[16,6144]{1,0:T(8,128)S(1)}, f32[16,6144]{1,0:T(8,128)S(1)}, u32[]{:S(2)}, u32[]{:S(2)}) %collective-permute-start.5) | collective-permute-done | bytes 393248 | tf_op jit(solution)/shard_map/ppermute | solution.py:166
  107.6 1.1 copy.20
  108.7 17.7 %collective-permute-done.6 = f32[16,6144]{1,0:T(8,128)} collective-permute-done((f32[16,6144]{1,0:T(8,128)S(1)}, f32[16,6144]{1,0:T(8,128)}, u32[]{:S(2)}, u32[]{:S(2)}) %collective-permute-start.6) | collective-permute-done | bytes 393248 | tf_op jit(solution)/shard_map/ppermute | solution.py:166
  126.4 1.2 pad_maximum_fusion
  128.3 3.4 fusion.79
  131.7 1.4 fusion.78
  133.1 26.5 %all-reduce = (f32[64,64]{1,0:T(8,128)S(1)}, f32[64,64]{1,0:T(8,128)S(1)}) all-reduce(f32[64,64]{1,0:T(8,128)S(1)} %fusion.78, f32[64,64]{1,0:T(8,128)S(1)} %fusion.79), channel_id=1, replica_groups=mesh['grp'=4,'slab'=8] {'slab'}, use_global_device_ids=true, to_apply=%region_8.9 | all-reduce | flops 8192 | bytes 65536 | tf_op jit(solution)/shard_map/psum | solution.py:194
  159.7 101.2 %while.63 = (s32[]{:T(128)}, f32[64,64]{1,0:T(8,128)S(1)}, f32[64,64]{0,1:T(8,128)S(1)}, s32[]{:T(128)}, s32[]{:T(128)}) while((s32[]{:T(128)}, f32[64,64]{1,0:T(8,128)S(1)}, f32[64,64]{0,1:T(8,128)S(1)}, s32[]{:T(128)}, s32[]{:T(128)}) %tuple.153), condition=%wide.region_7.8_spmd.clone.clone, body=%wide.region_6.7_spmd.clone.clone.sunk | while | flops 65923 | bytes 101992 | solution.py:72
  260.9 91.3 %while.60 = (s32[]{:T(128)}, f32[64,64]{1,0:T(8,128)S(1)}, f32[64,64]{1,0:T(8,128)S(1)}, f32[64,64]{1,0:T(8,128)S(1)}, s32[]{:T(128)}, /*index=5*/s32[]{:T(128)}, s32[]{:T(128)}) while((s32[]{:T(128)}, f32[64,64]{1,0:T(8,128)S(1)}, f32[64,64]{1,0:T(8,128)S(1)}, f32[64,64]{1,0:T(8,128)S(1)}, s32[]{:T(128)}, /*index=5*/s32[]{:T(128)}, ...), condition=%wide.region_10.11_spmd, body=%wide.region_9.10_spmd.sunk | while | flops 49283 | bytes 36205 | solution.py:89
  352.3 91.8 %while.61 = (s32[]{:T(128)}, f32[64,64]{1,0:T(8,128)S(1)}, f32[64,64]{1,0:T(8,128)S(1)}, f32[64,64]{0,1:T(8,128)S(1)}, s32[]{:T(128)}, /*index=5*/s32[]{:T(128)}, s32[]{:T(128)}, s32[]{:T(128)}) while((s32[]{:T(128)}, f32[64,64]{1,0:T(8,128)S(1)}, f32[64,64]{1,0:T(8,128)S(1)}, f32[64,64]{0,1:T(8,128)S(1)}, s32[]{:T(128)}, ...), condition=%wide.region_12.13_spmd, body=%wide.region_11.12_spmd.sunk | while | flops 49287 | bytes 35751 | solution.py:107
  444.1 2.9 fusion.26
  (905 shorter events, 276.2 us)
Async XLA Ops:
  6.5 121.7 %all-gather.3.cloned.1.call-start = ((), (), s32[]{:S(2)}) async-start(), calls=%async_computation | async-start | bytes 1966080 | tf_op jit(solution)/shard_map/all_gather | solution.py:190
  8.1 13.7 %collective-permute-start = (f32[16,1,8,128]{3,2,1,0:T(8,128)}, f32[16,1,8,128]{3,2,1,0:T(8,128)}, u32[]{:S(2)}, u32[]{:S(2)}) collective-permute-start(f32[16,1,8,128]{3,2,1,0:T(8,128)} %get-tuple-element.525), channel_id=1, source_target_pairs={{0,1},{1,2},{2,3},{3,4},{4,5},{5,6},{6,7},{8,9},{9,10},{10,11},{11... | collective-permute-start | bytes 196616 | tf_op jit(solution)/shard_map/ppermute | solution.py:27
  11.1 10.7 %collective-permute-start.1 = (f32[16,1,8,128]{3,2,1,0:T(8,128)}, f32[16,1,8,128]{3,2,1,0:T(8,128)}, u32[]{:S(2)}, u32[]{:S(2)}) collective-permute-start(f32[16,1,8,128]{3,2,1,0:T(8,128)} %get-tuple-element.526), channel_id=1, source_target_pairs={{1,0},{2,1},{3,2},{4,3},{5,4},{6,5},{7,6},{9,8},{10,9},{11,10},{12... | collective-permute-start | bytes 196616 | tf_op jit(solution)/shard_map/ppermute | solution.py:28
  24.2 9.3 %copy-start.6 = (f32[8,8,128]{2,1,0:T(8,128)S(1)}, f32[8,8,128]{2,1,0:T(8,128)}, u32[]{:S(2)}) copy-start(f32[8,8,128]{2,1,0:T(8,128)} %get-tuple-element.529) | copy-start | bytes 98308
  24.2 9.3 %copy-start.7 = (f32[8,8,128]{2,1,0:T(8,128)S(1)}, f32[8,8,128]{2,1,0:T(8,128)}, u32[]{:S(2)}) copy-start(f32[8,8,128]{2,1,0:T(8,128)} %get-tuple-element.530) | copy-start | bytes 98308
  24.2 9.3 %copy-start.8 = (f32[8,8,128]{2,1,0:T(8,128)S(1)}, f32[8,8,128]{2,1,0:T(8,128)}, u32[]{:S(2)}) copy-start(f32[8,8,128]{2,1,0:T(8,128)} %get-tuple-element.531) | copy-start | bytes 98308
  24.2 9.3 %copy-start.9 = (f32[8,8,128]{2,1,0:T(8,128)S(1)}, f32[8,8,128]{2,1,0:T(8,128)}, u32[]{:S(2)}) copy-start(f32[8,8,128]{2,1,0:T(8,128)} %get-tuple-element.532) | copy-start | bytes 98308
  24.2 9.3 %copy-start.10 = (f32[8,8,128]{2,1,0:T(8,128)S(1)}, f32[8,8,128]{2,1,0:T(8,128)}, u32[]{:S(2)}) copy-start(f32[8,8,128]{2,1,0:T(8,128)} %get-tuple-element.533) | copy-start | bytes 98308
  24.2 9.3 %copy-start.11 = (f32[8,8,128]{2,1,0:T(8,128)S(1)}, f32[8,8,128]{2,1,0:T(8,128)}, u32[]{:S(2)}) copy-start(f32[8,8,128]{2,1,0:T(8,128)} %get-tuple-element.534) | copy-start | bytes 98308
  24.5 6.0 %collective-permute-start.2 = (f32[16,1,8,128]{3,2,1,0:T(8,128)S(1)}, f32[16,1,8,128]{3,2,1,0:T(8,128)S(1)}, u32[]{:S(2)}, u32[]{:S(2)}) collective-permute-start(f32[16,1,8,128]{3,2,1,0:T(8,128)S(1)} %get-tuple-element.515), channel_id=1, source_target_pairs={{0,1},{1,2},{2,3},{3,4},{4,5},{5,6},{6,7},{8,9},{9,10},{10,11},{11... | collective-permute-start | bytes 196616 | tf_op jit(solution)/shard_map/ppermute | solution.py:27
  29.1 4.4 collective-permute-start.3
  34.4 31.2 %copy-start.13 = (f32[12,512]{1,0:T(8,128)S(1)}, f32[12,512]{1,0:T(8,128)}, u32[]{:S(2)}) copy-start(f32[12,512]{1,0:T(8,128)} %fusion.61) | copy-start | bytes 73732
  34.4 31.2 %copy-start.14 = (f32[12,512]{1,0:T(8,128)S(1)}, f32[12,512]{1,0:T(8,128)}, u32[]{:S(2)}) copy-start(f32[12,512]{1,0:T(8,128)} %div.111) | copy-start | bytes 73732
  34.4 47.7 %copy-start.15 = (f32[6144]{0:T(1024)S(1)}, f32[6144]{0:T(1024)}, u32[]{:S(2)}) copy-start(f32[6144]{0:T(1024)} %param.22) | copy-start | bytes 73732
  34.4 47.7 %copy-start.16 = (f32[6144]{0:T(1024)S(1)}, f32[6144]{0:T(1024)}, u32[]{:S(2)}) copy-start(f32[6144]{0:T(1024)} %fusion.62) | copy-start | bytes 73732
  34.4 47.7 %copy-start.17 = (f32[6144]{0:T(1024)S(1)}, f32[6144]{0:T(1024)}, u32[]{:S(2)}) copy-start(f32[6144]{0:T(1024)} %param.21) | copy-start | bytes 73732
  65.4 42.1 %copy-start.2 = (f32[16,64,128]{2,1,0:T(8,128)}, f32[16,64,128]{2,1,0:T(8,128)S(1)}, u32[]{:S(2)}) copy-start(f32[16,64,128]{2,1,0:T(8,128)S(1)} %get-tuple-element.711) | copy-start | bytes 1572868
  65.5 16.6 %copy-start.5 = (f32[16,6144]{1,0:T(8,128)S(1)}, f32[16,6144]{1,0:T(8,128)}, u32[]{:S(2)}) copy-start(f32[16,6144]{1,0:T(8,128)} %param.23) | copy-start | bytes 1179652
  83.0 361.0 %all-gather.5.cloned.1.call-start = ((), (), s32[]{:S(2)}) async-start(), calls=%async_computation.1 | async-start | bytes 2621440 | tf_op jit(solution)/shard_map/all_gather | solution.py:200
  83.1 11.2 %collective-permute-start.4 = (f32[16,6144]{1,0:T(8,128)S(1)}, f32[16,6144]{1,0:T(8,128)S(1)}, u32[]{:S(2)}, u32[]{:S(2)}) collective-permute-start(f32[16,6144]{1,0:T(8,128)S(1)} %get-tuple-element.527), channel_id=1, source_target_pairs={{0,8},{8,16},{16,24},{24,0},{1,9},{9,17},{17,25},{25,1},{2,10},{10... | collective-permute-start | bytes 1179656 | tf_op jit(solution)/shard_map/ppermute | solution.py:166
  94.3 13.2 %collective-permute-start.5 = (f32[16,6144]{1,0:T(8,128)S(1)}, f32[16,6144]{1,0:T(8,128)S(1)}, u32[]{:S(2)}, u32[]{:S(2)}) collective-permute-start(f32[16,6144]{1,0:T(8,128)S(1)} %collective-permute-done.4), channel_id=1, source_target_pairs={{0,8},{8,16},{16,24},{24,0},{1,9},{9,17},{17,25},{25,1},{2,10},{10... | collective-permute-start | bytes 1179656 | tf_op jit(solution)/shard_map/ppermute | solution.py:166
  107.5 18.8 %copy-start.4 = (f32[16,6144]{1,0:T(8,128)}, f32[16,6144]{1,0:T(8,128)S(1)}, u32[]{:S(2)}) copy-start(f32[16,6144]{1,0:T(8,128)S(1)} %collective-permute-done.5) | copy-start | bytes 1179652
  107.5 18.8 %collective-permute-start.6 = (f32[16,6144]{1,0:T(8,128)S(1)}, f32[16,6144]{1,0:T(8,128)}, u32[]{:S(2)}, u32[]{:S(2)}) collective-permute-start(f32[16,6144]{1,0:T(8,128)S(1)} %collective-permute-done.5), channel_id=1, source_target_pairs={{0,8},{8,16},{16,24},{24,0},{1,9},{9,17},{17,25},{25,1},{2,10},{10... | collective-permute-start | bytes 1179656 | tf_op jit(solution)/shard_map/ppermute | solution.py:166
  133.1 310.9 %copy-start.3 = (f32[16,64,128]{2,1,0:T(8,128)S(1)}, f32[16,64,128]{2,1,0:T(8,128)}, u32[]{:S(2)}) copy-start(f32[16,64,128]{2,1,0:T(8,128)} %copy-done.2) | copy-start | bytes 1572868
  (3 other events, 19.9 us)
Sparse Core Ops, SparseCore 0:
  83.1 41.4 all-gather.2
  126.5 34.4 all-gather.4
